TPU v7x, 256 devices: a whole 4x4x8 slice. The times are simulated.
256 devices in a mesh: mode: 8 (over z_hi, y), space: 32 (over x, z_lo, core).
Axes of the slice: x: 4, y: 4, z: 8 (z_hi: 2, z_lo: 4; z = z_hi * 4 + z_lo), core: 2. Of those that a mesh axis runs over, the one named last changes fastest.
Arguments:
- energy: float32 [128, 256, 16, 128], P('mode', 'space'), may hold values from -6 to 6
- void: int32 [256, 16, 128], P('space'), may hold values 0 or 1
- spacing_cells: float32 [256, 16, 128], P('space'), may hold values from 2 to 50
- walls: int32 [2, 256, 128], P(None, 'space'), may hold values from 0 to 2
- octant: int32 [128], replicated, may hold values from 0 to 7
- specific_warmth_modes: float32 [128], replicated, may hold values from 0.2 to 2
- second_derivative: float32 [128], replicated, may hold values from 0.5 to 1.5
- umklapp: float32 [128], replicated, may hold values from 0.02 to 1
- isotope: float32 [128], replicated, may hold values from 0.01 to 0.3
- courant: float32 [3, 128], replicated, may hold values from 0.05 to 0.9
Outputs:
- final_energy: float32 [128, 256, 16, 128], P('mode', 'space')
- prior_pseudo_kelvin: float32 [256, 16, 128], P('space')
Inputs may be any that keep to these rules, and one draw needn't show every extreme that they name: `walls`: 0 adiabatic wall, 1 cold black wall, 2 hot black wall. `octant`: bit 0, 1 and 2 give a negative direction along the first, second and third dimension.
All inputs are finite; a program needn't handle non-finite values. No bound on the sum of `void` on one device may be relied on, other than what follows from the above.
Results may differ from a plain program's by a relative error of at most 0.0003.
Values sent between devices are 32-bit elements; how exact they have to be, the bound alone decides.
A program may use at most 64 MiB of HBM per device.

v0:
```python
import jax
import jax.numpy as jnp
from jax import lax
from jax.sharding import PartitionSpec as P

ITERS = 8


RELAX_WEIGHT = 0.35
HOT_WALL = 1.0


def with_halo(cells, sides, width):
    for axis, dim in sides:
        count = lax.axis_size(axis)
        head = lax.slice_in_dim(cells, 0, width, axis=dim)
        tail = lax.slice_in_dim(cells, cells.shape[dim] - width, cells.shape[dim], axis=dim)
        cells = jnp.concatenate(
            [
                lax.ppermute(tail, axis, [(i, (i + 1) % count) for i in range(count)]),
                cells,
                lax.ppermute(head, axis, [((i + 1) % count, i) for i in range(count)]),
            ],
            axis=dim,
        )
    return cells


def broadcast_modes(vector):
    return vector[:, None, None, None]


def mode_signs(octant):
    sign_x = 1 - 2 * (octant % 2)
    sign_y = 1 - 2 * (octant // 2 % 2)
    sign_z = 1 - 2 * (octant // 4)
    return (sign_x, sign_y, sign_z)


def transfer_rate(umklapp, isotope, speed, spacing_cells):
    rate = broadcast_modes(umklapp + isotope) + broadcast_modes(speed) / spacing_cells[None]
    return 1.0 - jnp.exp(-rate)


def rest_population(specific_warmth_modes, second_derivative, prior_pseudo_kelvin):
    weighted_quantity = broadcast_modes(second_derivative) * prior_pseudo_kelvin[None]
    return (
        broadcast_modes(specific_warmth_modes / second_derivative) * jnp.sinh(weighted_quantity),
        broadcast_modes(specific_warmth_modes) * jnp.cosh(weighted_quantity),
    )


def beam_update(field, near, far, courant_band):
    factor = broadcast_modes(courant_band)
    return (
        field
        - 0.5 * factor * (3.0 * field - 4.0 * near + far)
        + 0.5 * factor * factor * (field - 2.0 * near + far)
    )


def beam_rolled(field, courant_band, sign, axis):
    forward = broadcast_modes(sign) > 0
    near = jnp.where(forward, jnp.roll(field, 1, axis), jnp.roll(field, -1, axis))
    far = jnp.where(forward, jnp.roll(field, 2, axis), jnp.roll(field, -2, axis))
    return beam_update(field, near, far, courant_band)


def wall_sweep(field, courant_band, sign, walls, specific_warmth_modes, second_derivative):
    factor = broadcast_modes(courant_band)
    forward = broadcast_modes(sign) > 0
    inflow = broadcast_modes(
        specific_warmth_modes / second_derivative * jnp.sinh(second_derivative * HOT_WALL)
    )
    bottom = jnp.where(walls[0] == 2, 1.0, 0.0)[None, :, None, :] * inflow
    upper = jnp.where(walls[1] == 2, 1.0, 0.0)[None, :, None, :] * inflow
    from_below = jnp.concatenate([bottom, field[:, :, :-1]], axis=2)
    from_above = jnp.concatenate([field[:, :, 1:], upper], axis=2)
    upstream = jnp.where(forward, from_below, from_above)
    depth = lax.broadcasted_iota(jnp.int32, (1, 1, field.shape[2], 1), 2)
    block_top = (depth == field.shape[2] - 1) & (walls[1] == 0)[None, :, None, :]
    block_bottom = (depth == 0) & (walls[0] == 0)[None, :, None, :]
    blocked = jnp.where(forward, block_top, block_bottom)
    outflow = jnp.where(blocked, 0.0, factor * field)
    return field - outflow + factor * upstream


def local(
    energy,
    void,
    spacing_cells,
    walls,
    octant,
    specific_warmth_modes,
    second_derivative,
    umklapp,
    isotope,
    courant,
):
    band_count = energy.shape[0]
    first_band = lax.axis_index("mode") * band_count

    def own_bands(table):
        return lax.dynamic_slice_in_dim(table, first_band, band_count, table.ndim - 1)

    fluid = (1 - void).astype(jnp.float32)
    sign_x, sign_y, sign_z = mode_signs(own_bands(octant))
    speed_all = jnp.sqrt(jnp.sum(courant * courant, axis=0))
    local_specific_warmth = own_bands(specific_warmth_modes)
    local_second_derivative = own_bands(second_derivative)
    own_courant = own_bands(courant)
    relax = transfer_rate(
        own_bands(umklapp), own_bands(isotope), own_bands(speed_all), spacing_cells
    )
    iterate_carry = energy * fluid[None]
    prior_pseudo_kelvin = jnp.zeros(spacing_cells.shape, jnp.float32)
    for sweep in range(ITERS):
        matrix_element, derivative_of_content = rest_population(
            local_specific_warmth, local_second_derivative, prior_pseudo_kelvin
        )
        balance_mismatch, combined_derivative = lax.psum(
            (
                jnp.sum(relax * (matrix_element - iterate_carry), axis=0),
                jnp.sum(relax * derivative_of_content, axis=0),
            ),
            "mode",
        )
        prior_pseudo_kelvin = (
            prior_pseudo_kelvin - RELAX_WEIGHT * balance_mismatch / combined_derivative
        )
    matrix_element, derivative_of_content = rest_population(
        local_specific_warmth, local_second_derivative, prior_pseudo_kelvin
    )
    iterate_carry = iterate_carry + relax * (matrix_element - iterate_carry)
    padded = with_halo(iterate_carry, (("space", 1),), 2)
    width = iterate_carry.shape[1]
    forward = broadcast_modes(sign_x) > 0
    near = jnp.where(forward, padded[:, 1 : 1 + width], padded[:, 3 : 3 + width])
    far = jnp.where(forward, padded[:, 0:width], padded[:, 4 : 4 + width])
    iterate_carry = beam_update(iterate_carry, near, far, own_courant[0])
    iterate_carry = wall_sweep(
        iterate_carry, own_courant[2], sign_z, walls, local_specific_warmth, local_second_derivative
    )
    iterate_carry = beam_rolled(iterate_carry, own_courant[1], sign_y, 3)
    iterate_carry = iterate_carry * fluid[None]
    return (iterate_carry, prior_pseudo_kelvin)


def solution(mesh):
    in_specs = (
        P("mode", "space", None, None),
        P("space", None, None),
        P("space", None, None),
        P(None, "space", None),
        P(),
        P(),
        P(),
        P(),
        P(),
        P(),
    )
    out_specs = (P("mode", "space", None, None), P("space", None, None))
    return jax.shard_map(local, mesh=mesh, in_specs=in_specs, out_specs=out_specs, check_vma=False)
```

profile of v0, /device:TPU:2, one launch (start us, length us, event | category | flops | bytes accessed | tf_op | source)
XLA Modules:
  0.0 884.6 jit_solution(9419108738488289381)
XLA Ops:
  7.2 0.8 multiply_reduce_fusion.2
  8.0 0.1 dynamic_slice.23
  8.1 0.8 fusion.150
  8.9 0.8 subtract_convert_fusion
  9.8 2.4 multiply_reduce_fusion.1
  12.2 0.0 all-reduce.29.cloned.1.call-start
  12.3 110.1 %all-reduce.31.cloned.1.call-done = (f32[8,16,128]{2,1,0:T(8,128)}, f32[8,16,128]{2,1,0:T(8,128)}) async-done(((f32[8,16,128]{2,1,0:T(8,128)}, f32[8,16,128]{2,1,0:T(8,128)}), (f32[8,16,128]{2,1,0:T(8,128)}, f32[8,16,128]{2,1,0:T(8,128)})) %all-reduce.31.cloned.1.call-update) | async-done | bytes 131088 | tf_op jit(solution)/shard_map/psum | solution.py:121
  122.3 0.9 divide_subtract_fusion.7
  123.3 2.1 fusion.140
  125.4 0.0 all-reduce.27.cloned.1.call-start
  125.5 102.3 %all-reduce.29.cloned.1.call-done = (f32[8,16,128]{2,1,0:T(8,128)}, f32[8,16,128]{2,1,0:T(8,128)}) async-done(((f32[8,16,128]{2,1,0:T(8,128)}, f32[8,16,128]{2,1,0:T(8,128)}), (f32[8,16,128]{2,1,0:T(8,128)}, f32[8,16,128]{2,1,0:T(8,128)})) %all-reduce.29.cloned.1.call-update) | async-done | bytes 131088 | tf_op jit(solution)/shard_map/psum | solution.py:121
  227.8 0.9 divide_subtract_fusion.6
  228.7 2.1 fusion.139
  231.0 102.4 %all-reduce.27.cloned.1.call-done = (f32[8,16,128]{2,1,0:T(8,128)}, f32[8,16,128]{2,1,0:T(8,128)}) async-done(((f32[8,16,128]{2,1,0:T(8,128)}, f32[8,16,128]{2,1,0:T(8,128)}), (f32[8,16,128]{2,1,0:T(8,128)}, f32[8,16,128]{2,1,0:T(8,128)})) %all-reduce.27.cloned.1.call-update) | async-done | bytes 131088 | tf_op jit(solution)/shard_map/psum | solution.py:121
  333.4 0.9 divide_subtract_fusion.5
  334.3 2.1 fusion.138
  336.5 102.3 %all-reduce.25.cloned.1.call-done = (f32[8,16,128]{2,1,0:T(8,128)}, f32[8,16,128]{2,1,0:T(8,128)}) async-done(((f32[8,16,128]{2,1,0:T(8,128)}, f32[8,16,128]{2,1,0:T(8,128)}), (f32[8,16,128]{2,1,0:T(8,128)}, f32[8,16,128]{2,1,0:T(8,128)})) %all-reduce.25.cloned.1.call-update) | async-done | bytes 131088 | tf_op jit(solution)/shard_map/psum | solution.py:121
  438.8 0.9 divide_subtract_fusion.4
  439.7 2.1 fusion.137
  442.0 0.1 broadcast_and_fusion
  442.1 102.2 %all-reduce.23.cloned.1.call-done = (f32[8,16,128]{2,1,0:T(8,128)}, f32[8,16,128]{2,1,0:T(8,128)}) async-done(((f32[8,16,128]{2,1,0:T(8,128)}, f32[8,16,128]{2,1,0:T(8,128)}), (f32[8,16,128]{2,1,0:T(8,128)}, f32[8,16,128]{2,1,0:T(8,128)})) %all-reduce.23.cloned.1.call-update) | async-done | bytes 131088 | tf_op jit(solution)/shard_map/psum | solution.py:121
  544.3 0.9 divide_subtract_fusion.3
  545.2 2.1 fusion.136
  547.4 0.0 all-reduce.19.cloned.1.call-start
  547.4 0.1 constant_dynamic-slice_fusion
  547.5 102.2 %all-reduce.21.cloned.1.call-done = (f32[8,16,128]{2,1,0:T(8,128)}, f32[8,16,128]{2,1,0:T(8,128)}) async-done(((f32[8,16,128]{2,1,0:T(8,128)}, f32[8,16,128]{2,1,0:T(8,128)}), (f32[8,16,128]{2,1,0:T(8,128)}, f32[8,16,128]{2,1,0:T(8,128)})) %all-reduce.21.cloned.1.call-update) | async-done | bytes 131088 | tf_op jit(solution)/shard_map/psum | solution.py:121
  649.7 0.9 divide_subtract_fusion.2
  650.6 2.1 fusion.135
  652.8 0.2 all-reduce.17.cloned.1.call-start
  653.0 102.2 %all-reduce.19.cloned.1.call-done = (f32[8,16,128]{2,1,0:T(8,128)}, f32[8,16,128]{2,1,0:T(8,128)}) async-done(((f32[8,16,128]{2,1,0:T(8,128)}, f32[8,16,128]{2,1,0:T(8,128)}), (f32[8,16,128]{2,1,0:T(8,128)}, f32[8,16,128]{2,1,0:T(8,128)})) %all-reduce.19.cloned.1.call-update) | async-done | bytes 131088 | tf_op jit(solution)/shard_map/psum | solution.py:121
  755.2 0.9 divide_subtract_fusion.1
  756.1 2.1 fusion.134
  758.3 0.1 fusion.148
  758.4 102.3 %all-reduce.17.cloned.1.call-done = (f32[8,16,128]{2,1,0:T(8,128)}, f32[8,16,128]{2,1,0:T(8,128)}) async-done(((f32[8,16,128]{2,1,0:T(8,128)}, f32[8,16,128]{2,1,0:T(8,128)}), (f32[8,16,128]{2,1,0:T(8,128)}, f32[8,16,128]{2,1,0:T(8,128)})) %all-reduce.17.cloned.1.call-update) | async-done | bytes 131088 | tf_op jit(solution)/shard_map/psum | solution.py:121
  860.7 0.9 divide_subtract_fusion
  861.6 1.3 fusion.130
  863.0 0.1 collective-permute-start
  863.0 4.4 collective-permute-start.1
  867.5 0.1 broadcast_multiply_fusion
  867.6 5.1 collective-permute-done
  872.8 0.6 multiply_add_fusion.8
  873.3 0.2 fusion.156
  873.6 0.5 fusion.133
  874.1 0.4 fusion.155
  874.5 0.4 fusion.154
  874.8 0.4 fusion.153
  875.2 0.4 fusion.152
  875.6 2.2 add_multiply_fusion
  (36 shorter events, 0.4 us)
Async XLA Ops:
  7.2 116.1 %copy-start.1 = (f32[8,16,128]{2,1,0:T(8,128)S(1)}, f32[8,16,128]{2,1,0:T(8,128)}, u32[]{:S(2)}) copy-start(f32[8,16,128]{2,1,0:T(8,128)} %param.12) | copy-start | bytes 196612
  7.2 116.1 %copy-start = (f32[16,8,16,128]{3,2,1,0:T(8,128)S(1)}, f32[16,8,16,128]{3,2,1,0:T(8,128)}, u32[]{:S(2)}) copy-start(f32[16,8,16,128]{3,2,1,0:T(8,128)} %param.10) | copy-start | bytes 3145732
  7.2 115.2 %all-reduce.31.cloned.1.call-start = ((), (), s32[]{:S(2)}) async-start(), calls=%async_computation.7 | async-start | bytes 262144 | tf_op jit(solution)/shard_map/psum | solution.py:121
  12.2 215.6 %all-reduce.29.cloned.1.call-start = ((), (), s32[]{:S(2)}) async-start(), calls=%async_computation.6 | async-start | bytes 262144 | tf_op jit(solution)/shard_map/psum | solution.py:121
  125.4 208.0 %all-reduce.27.cloned.1.call-start = ((), (), s32[]{:S(2)}) async-start(), calls=%async_computation.5 | async-start | bytes 262144 | tf_op jit(solution)/shard_map/psum | solution.py:121
  228.7 2.2 copy-start.3
  230.9 208.0 %all-reduce.25.cloned.1.call-start = ((), (), s32[]{:S(2)}) async-start(), calls=%async_computation.4 | async-start | bytes 262144 | tf_op jit(solution)/shard_map/psum | solution.py:121
  336.5 207.8 %all-reduce.23.cloned.1.call-start = ((), (), s32[]{:S(2)}) async-start(), calls=%async_computation.3 | async-start | bytes 262144 | tf_op jit(solution)/shard_map/psum | solution.py:121
  441.9 207.8 %all-reduce.21.cloned.1.call-start = ((), (), s32[]{:S(2)}) async-start(), calls=%async_computation.2 | async-start | bytes 262144 | tf_op jit(solution)/shard_map/psum | solution.py:121
  545.2 2.2 copy-start.4
  547.4 207.8 %all-reduce.19.cloned.1.call-start = ((), (), s32[]{:S(2)}) async-start(), calls=%async_computation.1 | async-start | bytes 262144 | tf_op jit(solution)/shard_map/psum | solution.py:121
  652.8 207.9 %all-reduce.17.cloned.1.call-start = ((), (), s32[]{:S(2)}) async-start(), calls=%async_computation | async-start | bytes 262144 | tf_op jit(solution)/shard_map/psum | solution.py:121
  756.1 2.2 copy-start.5
  861.6 1.3 copy-start.2
  863.0 9.8 %collective-permute-start = (f32[16,2,16,128]{3,2,1,0:T(8,128)S(1)}, f32[16,2,16,128]{3,2,1,0:T(8,128)S(1)}, u32[]{:S(2)}, u32[]{:S(2)}) collective-permute-start(f32[16,2,16,128]{3,2,1,0:T(8,128)S(1)} %get-tuple-element.50), channel_id=1, source_target_pairs={{0,1},{1,2},{2,3},{3,4},{4,5},{5,6},{6,7},{7,8},{8,9},{9,10},{10,1... | collective-permute-start | bytes 786440 | tf_op jit(solution)/shard_map/ppermute | solution.py:20
  863.0 9.7 %collective-permute-start.1 = (f32[16,2,16,128]{3,2,1,0:T(8,128)S(1)}, f32[16,2,16,128]{3,2,1,0:T(8,128)S(1)}, u32[]{:S(2)}, u32[]{:S(2)}) collective-permute-start(f32[16,2,16,128]{3,2,1,0:T(8,128)S(1)} %get-tuple-element.51), channel_id=1, source_target_pairs={{1,0},{2,1},{3,2},{4,3},{5,4},{6,5},{7,6},{8,7},{9,8},{10,9},{11,1... | collective-permute-start | bytes 786440 | tf_op jit(solution)/shard_map/ppermute | solution.py:22
Sparse Core Ops, SparseCore 0:
  12.3 109.9 all-reduce.30
  125.6 102.2 all-reduce.28
  231.0 102.3 all-reduce.26
  336.6 102.2 all-reduce.24
  442.0 102.2 all-reduce.22
  547.5 102.2 all-reduce.20
  653.0 102.2 all-reduce.18
  758.4 102.2 all-reduce.16
where the time goes:
time: 886 us; the launch traced here: 885 us
  waiting for transfers between devices  831 us (94%)
  other arithmetic  31.9 us (4%)
  between operations  14.4 us (2%)
    psum x8, waiting for transfers between devices, local(): lax.psum((jnp.sum(relax * (matrix_element - iterate_carry), axis=0), jnp....  826 us
  transfers between devices with their start and end apart: 10, of which 9 were waited for; matrix products, arithmetic and copies ran while one was open for 0% of the time, Pallas kernels for 0%

commit v1 on v0

v1 whole, which is shorter than its diff:
```python
import functools
import math

import jax
import jax.numpy as jnp
from jax import lax
from jax.experimental import pallas as pl
from jax.experimental.pallas import tpu as pltpu
from jax.sharding import PartitionSpec as P

MESH = pl.DeviceIdType.MESH
F32 = jnp.float32
ITERS = 8
RELAX_WEIGHT = 0.35
TERMS = 23
ROWS = 8
MIDDLE, HALF = 0.26, 0.24
TOP_CURVATURE = 1.5
REACH = 16.0
YS = 4


def place_of_layer(layer):
    return {0: (0, 0), 1: (1, 0), 6: (2, 0), 7: (3, 0), 2: (0, 1), 3: (1, 1), 4: (2, 1), 5: (3, 1)}[layer]


def sinh(x):
    square = x * x
    near_zero = x * (1.0 + square * (1 / 6 + square * (1 / 120 + square * (1 / 5040))))
    return jnp.where(jnp.abs(x) < 0.5, near_zero, 0.5 * (jnp.exp(x) - jnp.exp(-x)))


def splat(value):
    return jnp.full((8, 128), value, F32)


def kernel(
    spaces,
    energy,
    void,
    spacing,
    walls,
    octant,
    warmth,
    curvature,
    umklapp,
    isotope,
    courant,
    out_ref,
    temp_ref,
    e_v,
    void_v,
    space_v,
    walls_v,
    rows_v,
    courant_v,
    octant_s,
    warmth_s,
    curvature_s,
    umklapp_s,
    isotope_s,
    courant_s,
    inverse,
    fluid,
    keep,
    inflow_mask,
    kept,
    relax,
    part,
    part_in,
    total,
    total_in,
    temps,
    temps_in,
    halo_e,
    halo_void,
    halo_space,
    halo_relax,
    table_q,
    table_k,
    table_a,
    lifted,
    local_sem,
    part_send,
    part_recv,
    z_send,
    z_recv,
    t_send,
    t_recv,
    edge_send,
    edge_recv,
    halo_send,
    halo_recv,
):
    bands, layers = energy.shape[0], energy.shape[1]
    me_m, me_s = lax.axis_index("mode"), lax.axis_index("space")
    y, z = lax.rem(me_m, YS), lax.div(me_m, YS)
    first = me_m * bands
    right, left = lax.rem(me_s + 1, spaces), lax.rem(me_s + spaces - 1, spaces)
    peers = [z * YS + lax.rem(y + i, YS) for i in range(1, YS)]
    across = (1 - z) * YS + y

    groups = 4
    per = bands // groups
    loads = [
        pltpu.make_async_copy(src, dst, local_sem.at[i])
        for i, (src, dst) in enumerate(
            [
                (spacing, space_v),
                (void, void_v),
                (umklapp, umklapp_s),
                (isotope, isotope_s),
                (courant, courant_s),
            ]
            + [(energy.at[pl.ds(g * per, per)], e_v.at[pl.ds(g * per, per)]) for g in range(groups)]
            + [
                (warmth, warmth_s),
                (curvature, curvature_s),
                (octant, octant_s),
                (warmth, rows_v.at[0]),
                (curvature, rows_v.at[1]),
                (umklapp, rows_v.at[2]),
                (isotope, rows_v.at[3]),
                (courant, courant_v),
                (walls, walls_v),
            ]
        )
    ]
    for copy in loads:
        copy.start()

    barrier = pltpu.get_barrier_semaphore()

    def tell(mode, space):
        pl.semaphore_signal(barrier, inc=1, device_id={"mode": mode, "space": space}, device_id_type=MESH)

    for peer in peers:
        tell(peer, me_s)
    tell(across, me_s)
    tell(me_m, right)
    tell(me_m, left)
    tell(z * YS + 0, right)
    tell(z * YS + 1, right)
    tell(z * YS + 2, left)
    tell(z * YS + 3, left)

    for copy in loads[:5]:
        copy.wait()
    inverse[...] = 1.0 / space_v[...]
    fluid[...] = (1 - void_v[...]).astype(F32)

    def rates(band):
        c0, c1, c2 = (splat(courant_s[i, band]) for i in range(3))
        speed = jnp.sqrt(c0 * c0 + c1 * c1 + c2 * c2)
        return splat(umklapp_s[band]) + splat(isotope_s[band]), speed

    shares = [jnp.zeros((16, 128), F32) for _ in range(layers)]
    for g in range(groups):
        loads[5 + g].wait()

        def share(i, sums, g=g):
            b = g * per + i
            base, speed = rates(first + b)
            base, speed = jnp.tile(base, (2, 1)), jnp.tile(speed, (2, 1))
            new = []
            for layer in range(layers):
                left_over = jnp.exp(-(base + speed * inverse[layer]))
                state = e_v[b, layer] * fluid[layer]
                held = left_over * state
                kept[b, layer + 2] = held
                relax[b, layer] = 1.0 - left_over
                new.append(sums[layer] + (state - held))
            return new

        shares = lax.fori_loop(0, per, share, shares)
    for layer in range(layers):
        part[place_of_layer(layer)] = shares[layer]

    pl.semaphore_wait(barrier, 10)

    part_copies = [
        pltpu.make_async_remote_copy(
            src_ref=part.at[lax.rem(y + i, YS)],
            dst_ref=part_in.at[3 - i],
            send_sem=part_send.at[i - 1],
            recv_sem=part_recv.at[3 - i],
            device_id={"mode": peers[i - 1]},
            device_id_type=MESH,
        )
        for i in range(1, YS)
    ]
    for copy in part_copies:
        copy.start()

    halo_copies = []
    for side, (target, start) in enumerate(((right, layers - 2), (left, 0))):
        for i, (src, dst) in enumerate(
            (
                (energy.at[:, pl.ds(start, 2)], halo_e.at[side]),
                (spacing.at[pl.ds(start, 2)], halo_space.at[side]),
                (void.at[pl.ds(start, 2)], halo_void.at[side]),
            )
        ):
            halo_copies.append(
                pltpu.make_async_remote_copy(
                    src_ref=src,
                    dst_ref=dst,
                    send_sem=halo_send.at[side * 3 + i],
                    recv_sem=halo_recv.at[side * 3 + i],
                    device_id={"space": target},
                    device_id_type=MESH,
                )
            )
    for copy in halo_copies:
        copy.start()

    for copy in loads[5 + groups :]:
        copy.wait()
    warm_row, curve_row = rows_v[0:1, :], rows_v[1:2, :]
    c_rows = courant_v[...]
    speed_row = jnp.sqrt(jnp.sum(c_rows * c_rows, axis=0, keepdims=True))
    weight = jnp.exp(-(rows_v[2:3, :] + rows_v[3:4, :] + MIDDLE * speed_row))
    slant = HALF * speed_row
    power = jnp.ones_like(slant)
    powers = []
    for j in range(ROWS + 1):
        powers.append(power * (1.0 / math.factorial(j)))
        power = power * (-slant)
    fold = {0: -1 / 128, 2: 0.25, 4: -1.25, 6: 2.0}
    for j in range(ROWS):
        row = powers[j] + fold[j] * powers[ROWS] if j in fold else powers[j]
        row = -weight * row
        table_q[j : j + 1, :] = 1.0 + row if j == 0 else row
    q = table_q[...]
    ratio = curve_row * (1.0 / TOP_CURVATURE)
    ratio = jnp.broadcast_to(ratio * ratio, (8, 128))
    grown = jnp.broadcast_to(warm_row, (8, 128))
    for k in range(TERMS):
        factor = REACH ** (2 * k) / math.factorial(2 * k + 1)
        moment = jnp.sum(q * grown, axis=1, keepdims=True) * factor
        table_k[k] = jnp.broadcast_to(moment, (8, 128))
        grown = grown * ratio
    edge, inner = y + 4 * lax.div(y, 2), y + 2
    v = jnp.concatenate([inverse[edge], inverse[inner]], axis=0)
    v = (v - MIDDLE) * (1.0 / HALF)
    for k in range(TERMS):
        value = jnp.broadcast_to(table_k[k, ROWS - 1 : ROWS, :], v.shape)
        for j in range(ROWS - 2, -1, -1):
            value = value * v + table_k[k, j : j + 1, :]
        table_a[k] = value

    depth = lax.broadcasted_iota(jnp.int32, (16, 128), 0)
    for layer in range(layers):
        bottom, upper = walls_v[0, layer : layer + 1, :], walls_v[1, layer : layer + 1, :]
        inflow_mask[0, layer : layer + 1, :] = jnp.where(bottom == 2, 1.0, 0.0)
        inflow_mask[1, layer : layer + 1, :] = jnp.where(upper == 2, 1.0, 0.0)
        keep[0, layer] = jnp.where((depth == 15) & (upper == 0), 0.0, 1.0)
        keep[1, layer] = jnp.where((depth == 0) & (bottom == 0), 0.0, 1.0)

    for copy in part_copies:
        copy.wait_recv()
    total[...] = (part[y] + part_in[0]) + (part_in[1] + part_in[2])
    z_copy = pltpu.make_async_remote_copy(
        src_ref=total,
        dst_ref=total_in,
        send_sem=z_send,
        recv_sem=z_recv,
        device_id={"mode": across},
        device_id_type=MESH,
    )
    z_copy.start()
    z_copy.wait_recv()
    goal = (total[...] + total_in[...]).reshape(32, 128)

    def newton(_, temp):
        scaled = temp * (TOP_CURVATURE / REACH)
        square = scaled * scaled
        value = table_a[TERMS - 1]
        slope = jnp.zeros_like(value)
        for k in range(TERMS - 2, -1, -1):
            slope = slope * square + value
            value = value * square + table_a[k]
        slope = value + 2.0 * square * slope
        return temp - RELAX_WEIGHT * (temp * value - goal) / slope

    temp = RELAX_WEIGHT * goal / table_a[0]
    temp = lax.fori_loop(1, ITERS, newton, temp)
    temps[y] = temp.reshape(2, 16, 128)

    t_copies = [
        pltpu.make_async_remote_copy(
            src_ref=temps.at[y],
            dst_ref=temps.at[y],
            send_sem=t_send.at[i - 1],
            recv_sem=t_recv.at[3 - i],
            device_id={"mode": peers[i - 1]},
            device_id_type=MESH,
        )
        for i in range(1, YS)
    ]
    beside = lax.rem(me_s + spaces - 1 + 2 * lax.div(y, 2), spaces)
    slot = lax.rem(y + 2, YS)
    edge_copies = [
        pltpu.make_async_remote_copy(
            src_ref=temps.at[y, 0],
            dst_ref=temps_in.at[slot],
            send_sem=edge_send.at[i],
            recv_sem=edge_recv.at[slot],
            device_id={"mode": z * YS + i, "space": beside},
            device_id_type=MESH,
        )
        for i in range(YS)
    ]
    for copy in t_copies + edge_copies:
        copy.start()

    for copy in halo_copies:
        copy.wait_recv()

    def halo_share(b, _):
        base, speed = rates(first + b)
        base, speed = jnp.tile(base, (2, 1)), jnp.tile(speed, (2, 1))
        for side in range(2):
            for i in range(2):
                left_over = jnp.exp(-(base + speed / halo_space[side, i]))
                state = halo_e[side, b, i] * (1 - halo_void[side, i]).astype(F32)
                kept[b, side * (layers + 2) + i] = left_over * state
                halo_relax[b, side * 2 + i] = 1.0 - left_over
        return _

    lax.fori_loop(0, bands, halo_share, 0)

    for copy in t_copies:
        copy.wait_recv()
    for layer in range(layers):
        temp_ref[layer] = temps[place_of_layer(layer)]

    def equilibrium(band):
        bend = splat(curvature_s[band])
        scale = splat(warmth_s[band]) / bend
        return jnp.tile(bend, (2, 1)), jnp.tile(scale, (2, 1))

    def sweep(b, which, bend, scale):
        band = first + b
        kind = octant_s[band]
        back_x, back_y, back_z = kind & 1, (kind >> 1) & 1, (kind >> 2) & 1
        step_x = 1 - 2 * back_x
        cx, cy, cz = (jnp.full((16, 128), courant_s[i, band], F32) for i in range(3))
        x_near, x_far = cx * (2.0 - cx), cx * (0.5 * cx - 0.5)
        x_own = 1.0 - x_near - x_far
        y_near, y_far = cy * (2.0 - cy), cy * (0.5 * cy - 0.5)
        y_own = 1.0 - y_near - y_far
        inflow = (scale * sinh(bend))[0:1, :]
        for layer in which:
            own = kept[b, layer + 2]
            near = kept[b, layer + 2 - step_x]
            far = kept[b, layer + 2 - 2 * step_x]
            lifted[layer, 8:24, :] = x_own * own + x_near * near + x_far * far
            lifted[layer, 7:8, :] = inflow * inflow_mask[0, layer : layer + 1, :]
            lifted[layer, 24:25, :] = inflow * inflow_mask[1, layer : layer + 1, :]
        turn_near, turn_far = 1 + 126 * back_y, 2 + 124 * back_y
        for layer in which:
            field = lifted[layer, 8:24, :]
            upstream = lifted[layer, pl.ds(7 + 2 * back_z, 16), :]
            field = field - cz * keep[back_z, layer] * field + cz * upstream
            near = pltpu.roll(field, turn_near, 1)
            far = pltpu.roll(field, turn_far, 1)
            out_ref[b, layer] = (y_own * field + y_near * near + y_far * far) * fluid[layer]

    def inner_layers(b, _):
        bend, scale = equilibrium(first + b)
        for layer in range(layers):
            level = scale * sinh(bend * temps[place_of_layer(layer)])
            kept[b, layer + 2] = kept[b, layer + 2] + relax[b, layer] * level
        sweep(b, range(2, layers - 2), bend, scale)
        return _

    lax.fori_loop(0, bands, inner_layers, 0)

    for i in range(YS):
        pltpu.make_async_remote_copy(
            src_ref=temps.at[y, 0],
            dst_ref=temps_in.at[i],
            send_sem=edge_send.at[i],
            recv_sem=edge_recv.at[i],
            device_id={"mode": z * YS + i, "space": beside},
            device_id_type=MESH,
        ).wait_recv()

    def edge_layers(b, _):
        bend, scale = equilibrium(first + b)
        for i in range(4):
            at = i if i < 2 else layers + i
            level = scale * sinh(bend * temps_in[i])
            kept[b, at] = kept[b, at] + halo_relax[b, i] * level
        sweep(b, (0, 1, layers - 2, layers - 1), bend, scale)
        return _

    lax.fori_loop(0, bands, edge_layers, 0)

    for copy in part_copies + [z_copy] + t_copies + edge_copies + halo_copies:
        copy.wait_send()


def local(spaces, energy, void, spacing, walls, octant, warmth, curvature, umklapp, isotope, courant):
    bands, layers, deep, wide = energy.shape
    vmem = lambda *shape: pltpu.VMEM(shape, F32)
    dma = lambda *shape: pltpu.SemaphoreType.DMA(shape)
    return pl.pallas_call(
        functools.partial(kernel, spaces),
        out_shape=(
            jax.ShapeDtypeStruct(energy.shape, F32),
            jax.ShapeDtypeStruct(spacing.shape, F32),
        ),
        in_specs=[pl.BlockSpec(memory_space=pl.ANY)] * 10,
        out_specs=(pl.BlockSpec(memory_space=pltpu.VMEM),) * 2,
        scratch_shapes=[
            vmem(bands, layers, deep, wide),
            pltpu.VMEM((layers, deep, wide), jnp.int32),
            vmem(layers, deep, wide),
            pltpu.VMEM((2, layers, wide), jnp.int32),
            vmem(8, wide),
            vmem(3, wide),
            pltpu.SMEM((128,), jnp.int32),
            pltpu.SMEM((128,), F32),
            pltpu.SMEM((128,), F32),
            pltpu.SMEM((128,), F32),
            pltpu.SMEM((128,), F32),
            pltpu.SMEM((3, 128), F32),
            vmem(layers, deep, wide),
            vmem(layers, deep, wide),
            vmem(2, layers, deep, wide),
            vmem(2, layers, wide),
            vmem(bands, layers + 4, deep, wide),
            vmem(bands, layers, deep, wide),
            vmem(YS, 2, deep, wide),
            vmem(3, 2, deep, wide),
            vmem(2, deep, wide),
            vmem(2, deep, wide),
            vmem(YS, 2, deep, wide),
            vmem(YS, deep, wide),
            vmem(2, bands, 2, deep, wide),
            pltpu.VMEM((2, 2, deep, wide), jnp.int32),
            vmem(2, 2, deep, wide),
            vmem(bands, 4, deep, wide),
            vmem(8, wide),
            vmem(TERMS, 8, wide),
            vmem(TERMS, 32, wide),
            vmem(layers, 32, wide),
            dma(24),
            dma(3),
            dma(3),
            dma(),
            dma(),
            dma(3),
            dma(3),
            dma(4),
            dma(4),
            dma(6),
            dma(6),
        ],
        compiler_params=pltpu.CompilerParams(collective_id=0, has_side_effects=True),
        name="transport",
    )(energy, void, spacing, walls, octant, warmth, curvature, umklapp, isotope, courant)


def solution(mesh):
    in_specs = (
        P("mode", "space", None, None),
        P("space", None, None),
        P("space", None, None),
        P(None, "space", None),
        P(),
        P(),
        P(),
        P(),
        P(),
        P(),
    )
    out_specs = (P("mode", "space", None, None), P("space", None, None))
    return jax.shard_map(
        functools.partial(local, mesh.shape["space"]),
        mesh=mesh,
        in_specs=in_specs,
        out_specs=out_specs,
        check_vma=False,
    )
```

time: 886 us -> 32.9 us (0.04)
  waiting for transfers between devices: 831 us -> 0 us
  other arithmetic: 31.9 us -> 0 us
  Pallas kernels: 0 us -> 29.1 us
  between operations: 14.4 us -> 0.65 us
    psum x8 -> x0, waiting for transfers between devices: 826 us -> none  [local(): lax.psum((jnp.sum(relax * (matrix_element - iterate_carry), axis=0), jnp....]
    pallas_call x0 -> x1, Pallas kernels: none -> 29.1 us  [local(): pl.pallas_call(functools.partial(kernel, spaces), out_shape=(jax.ShapeDty...]
    reduce_sum x9 -> x0, other arithmetic: 18.2 us -> none  [the longest x8 17.4 us: local(): jnp.sum(relax * (matrix_element - iterate_carry), axis=0)]
  transfers between devices with their start and end apart: 10 -> 0, of which waited for: 9 -> 0; matrix products, arithmetic and copies ran while one was open for 0% -> 0% of each run, Pallas kernels for 0% -> 0%
where the time goes in v1:
time: 32.9 us; the launch traced here: 32.7 us
  Pallas kernels  29.1 us (88%)
  local copies, waits for them, and re-layouts  2.96 us (9%)
  between operations  0.65 us (2%)
    pallas_call x1, Pallas kernels, local(): pl.pallas_call(functools.partial(kernel, spaces), out_shape=(jax.ShapeDty...  29.1 us
    unnamed x4, local copies, waits for them, and re-layouts  2.96 us

profile of v1, /device:TPU:2, one launch (start us, length us, event | category | flops | bytes accessed | tf_op | source)
XLA Modules:
  0.0 32.7 jit_solution(17433396874760585472)
XLA Ops:
  0.6 29.1 %transport.1 = (f32[16,8,16,128]{3,2,1,0:T(8,128)}, f32[8,16,128]{2,1,0:T(8,128)}) custom-call(f32[16,8,16,128]{3,2,1,0:T(8,128)} %energy.1, s32[8,16,128]{2,1,0:T(8,128)} %void.1, f32[8,16,128]{2,1,0:T(8,128)} %spacing.1, s32[2,8,128]{2,1,0:T(8,128)} %walls.1, s32[128]{0:T(128)} %octant.1, f32[128]{0:T(128)} %warmth.1, f32[128]{0:T(128)} %curvature.1, ...), custom_call_target="tpu_custom_call" | custom-call | tf_op jit(solution)/shard_map/transport/pallas_call | solution.py:409
  29.8 0.0 copy-start
  29.8 2.3 %copy.14 = f32[16,8,16,128]{3,2,1,0:T(8,128)} copy(f32[16,8,16,128]{3,2,1,0:T(8,128)} %get-tuple-element.4) | data formatting | bytes 2097152
  32.1 0.0 copy-done
  32.1 0.6 %copy.15 = f32[8,16,128]{2,1,0:T(8,128)} copy(f32[8,16,128]{2,1,0:T(8,128)S(1)} %copy-done) | data formatting | bytes 131072
Async XLA Ops:
  29.8 2.3 %copy-start = (f32[8,16,128]{2,1,0:T(8,128)S(1)}, f32[8,16,128]{2,1,0:T(8,128)}, u32[]{:S(2)}) copy-start(f32[8,16,128]{2,1,0:T(8,128)} %get-tuple-element.5) | copy-start | bytes 196612
